TPU v7x, 32 devices: a whole 2x2x4 slice. The times are simulated.
32 devices in a mesh: domain: 2 (over x), fsdp: 16 (over z, y, core).
Axes of the slice: x: 2, y: 2, z: 4, core: 2. Of those that a mesh axis runs over, the one named last changes fastest.
Arguments:
- gradients: bfloat16 [2, 4, 4096, 512], P('domain', None, 'fsdp')
- row_counts: int32 [4], replicated, may hold values from 2048 to 4096, as said below
- domain_ids: int32 [2], replicated, may hold values from 0 to 7
- domain_weights: float32 [8], replicated, may hold values from 0.2 to 2
Outputs:
- updates: float32 [4, 4096, 512], P('domain', 'fsdp')
- new_weights: float32 [8], replicated
Inputs may be any that keep to these rules, and one draw needn't show every extreme that they name: `row_counts`: each matrix has 4096 or 2048 rows, and both counts occur.
All inputs are finite; a program needn't handle non-finite values.
Results may differ from a plain program's by a relative error of at most 0.0071.
Values may be sent and summed in bfloat16 or wider, within the bound.
No kernel may reach another device: no remote copies, remote signals or barrier semaphores. Data moves between devices by JAX's collectives and lax.ppermute only.
A program may use at most 64 MiB of HBM per device.

v0:
```python
import math
import jax
import jax.numpy as jnp
from jax import lax
from jax.sharding import PartitionSpec as P

NS_ITERS = 3
OWNERS = 8
COEF_A = 3.4445
COEF_B = -4.775
COEF_C = 2.0315
MUON_SCALE = 0.2
ETA = 4.0


def partner(shard, axis, stride):
    return lax.ppermute(shard, axis, [(i, i ^ 1 << stride) for i in range(lax.axis_size(axis))])


def group_mixing(domain_ids, domain_weights, kind_count):
    weight_share = domain_weights / jnp.sum(domain_weights)
    onehot = (domain_ids[:, None] == jnp.arange(kind_count, dtype=jnp.int32)[None, :]).astype(
        jnp.float32
    )
    counts = jnp.sum(onehot, axis=0)
    per_member = weight_share / jnp.maximum(counts, 1.0)
    group_mix = jnp.sum(onehot * per_member[None, :], axis=1)
    return (weight_share, onehot, counts, group_mix)


def summed_gram(iterate):
    gram_total = lax.dot_general(
        iterate, iterate, (((0,), (0,)), ((), ())), preferred_element_type=jnp.float32
    )
    for bit_pos in range(OWNERS.bit_length() - 1):
        gram_total = gram_total + partner(gram_total, "fsdp", bit_pos)
    return gram_total


def newton_steps(iterate):
    for repeat in range(NS_ITERS):
        gram_full = lax.optimization_barrier(summed_gram(iterate).astype(jnp.bfloat16))
        square = jnp.dot(gram_full, gram_full, preferred_element_type=jnp.float32)
        poly_term = (COEF_B * gram_full.astype(jnp.float32) + COEF_C * square).astype(jnp.bfloat16)
        iterate = lax.optimization_barrier(
            (
                COEF_A * iterate.astype(jnp.float32)
                + jnp.dot(iterate, poly_term, preferred_element_type=jnp.float32)
            ).astype(jnp.bfloat16)
        )
    return iterate


def share_scores(aligned, squares, norm_slots):
    return lax.psum((aligned, squares, norm_slots), ("domain", "fsdp"))


def body(gradients, row_counts, domain_ids, domain_weights):
    groups = lax.axis_size("domain")
    shards = lax.axis_size("fsdp")
    matrices = row_counts.shape[0]
    rows_src = gradients.shape[2]
    columns = gradients.shape[3]
    per_domain = matrices // groups
    sub_rows = rows_src // OWNERS
    own_rows = shards * sub_rows
    full_rows = rows_src * shards
    domain_pos = lax.axis_index("domain")
    shard_pos = lax.axis_index("fsdp")
    weight_share, onehot, counts, group_mix = group_mixing(
        domain_ids, domain_weights, domain_weights.shape[0]
    )
    blocks = lax.all_to_all(
        gradients.reshape(1, groups, per_domain, rows_src, columns),
        "domain",
        split_axis=1,
        concat_axis=0,
        tiled=True,
    )
    blocks = blocks.reshape(groups, per_domain, rows_src, columns)
    global_rows = shard_pos * rows_src + jnp.arange(rows_src, dtype=jnp.int32)
    limits = lax.dynamic_slice_in_dim(row_counts, domain_pos * per_domain, per_domain, 0)
    row_mask = (global_rows[None, :] < limits[:, None])[None, :, :, None]
    masked = jnp.where(row_mask, blocks.astype(jnp.float32), jnp.zeros((), jnp.float32))
    combined = jnp.sum(group_mix[:, None, None, None] * masked, axis=0)
    aligned = jnp.sum(masked * combined[None], axis=(1, 2, 3))
    squares = jnp.sum(masked * masked, axis=(1, 2, 3))
    block_squares = jnp.sum(combined * combined, axis=(1, 2))
    norm_slots = lax.dynamic_update_slice_in_dim(
        jnp.zeros((matrices,), jnp.float32), block_squares, domain_pos * per_domain, 0
    )
    aligned, squares, norm_slots = share_scores(aligned, squares, norm_slots)
    frob_norm = (
        jnp.sqrt(lax.dynamic_slice_in_dim(norm_slots, domain_pos * per_domain, per_domain, 0))
        + 1e-07
    )
    scaled = (combined / frob_norm[:, None, None]).astype(jnp.bfloat16)
    scaled = scaled.reshape(shards, 1, sub_rows, columns)
    start_rows = lax.all_to_all(scaled, "fsdp", split_axis=0, concat_axis=1, tiled=True)
    start_rows = lax.optimization_barrier(start_rows.reshape(own_rows, columns))
    finished = newton_steps(start_rows)
    returned = lax.all_to_all(
        finished.reshape(1, shards, sub_rows, columns),
        "fsdp",
        split_axis=1,
        concat_axis=0,
        tiled=True,
    )
    returned = returned.reshape(per_domain, rows_src, columns)
    updates = returned.astype(jnp.float32) * (MUON_SCALE * math.sqrt(full_rows))
    total_sq = jnp.sum(norm_slots)
    cosine = aligned / (jnp.sqrt(squares) * jnp.sqrt(total_sq) + 1e-06)
    score = jnp.sum(onehot * cosine[:, None], axis=0) / jnp.maximum(counts, 1.0)
    raised = weight_share * jnp.exp(ETA * score)
    return (updates, raised / jnp.sum(raised))


def solution(mesh):
    placed = (P("domain", None, "fsdp", None), P(), P(), P())
    return jax.shard_map(
        body,
        mesh=mesh,
        in_specs=placed,
        out_specs=(P("domain", "fsdp", None), P()),
        check_vma=False,
    )
```

profile of v0, /device:TPU:0, one launch (start us, length us, event | category | flops | bytes accessed | tf_op | source)
XLA Modules:
  0.0 265.7 jit_solution(6877497156156330844)
XLA Ops:
  0.7 4.4 %all-to-all-start = ((bf16[1,2,2,256,512]{4,3,2,0,1:T(8,128)(2,1)}), bf16[1,2,2,256,512]{4,3,2,0,1:T(8,128)(2,1)S(1)}, u32[]{:S(2)}, u32[]{:S(2)}) async-start(bf16[1,2,2,256,512]{4,3,2,0,1:T(8,128)(2,1)} %bitcast.31), calls=%async_computation | async-start | bytes 2097152 | tf_op jit(solution)/shard_map/all_to_all | solution.py:73
  6.7 12.7 %all-to-all-done = bf16[1,2,2,256,512]{4,3,2,0,1:T(8,128)(2,1)S(1)} async-done(((bf16[1,2,2,256,512]{4,3,2,0,1:T(8,128)(2,1)}), bf16[1,2,2,256,512]{4,3,2,0,1:T(8,128)(2,1)S(1)}, u32[]{:S(2)}, u32[]{:S(2)}) %all-to-all-start) | async-done | bytes 1048608 | tf_op jit(solution)/shard_map/all_to_all | solution.py:73
  20.9 39.8 %all-reduce = (f32[4]{0:T(128)S(1)}, f32[2]{0:T(128)S(1)}, f32[2]{0:T(128)S(1)}) all-reduce(f32[4]{0:T(128)S(1)} %dynamic_update_slice.3, f32[2]{0:T(128)S(1)} %get-tuple-element.3, f32[2]{0:T(128)S(1)} %get-tuple-element.2), channel_id=1, replica_groups=mesh['domain'=2,'fsdp'=16] {'domain','fsdp'}, use_global_device_ids=true, to_apply=%region_5.6 | all-reduce | flops 8 | bytes 64 | tf_op jit(solution)/shard_map/psum | solution.py:55
  62.4 19.5 %all_to_all.12 = bf16[16,1,32,512]{3,2,1,0:T(8,128)(2,1)S(1)} all-to-all(bf16[16,1,32,512]{3,2,1,0:T(8,128)(2,1)S(1)} %divide_convert_fusion), channel_id=1, replica_groups=mesh['domain'=2,'fsdp'=16] {'fsdp'}, dimensions={0} | all-to-all | bytes 1048576 | tf_op jit(solution)/shard_map/all_to_all | solution.py:99
  82.6 2.5 collective-permute-done
  86.4 24.2 %collective-permute-done.1 = f32[512,512]{1,0:T(8,128)S(1)} collective-permute-done((f32[512,512]{1,0:T(8,128)S(1)}, f32[512,512]{1,0:T(8,128)S(1)}, u32[]{:S(2)}, u32[]{:S(2)}) %collective-permute-start.1) | collective-permute-done | bytes 1048608 | tf_op jit(solution)/shard_map/ppermute | solution.py:17
  110.8 1.8 collective-permute-start.2
  112.6 22.8 %collective-permute-done.2 = f32[512,512]{1,0:T(8,128)S(1)} collective-permute-done((f32[512,512]{1,0:T(8,128)S(1)}, f32[512,512]{1,0:T(8,128)S(1)}, u32[]{:S(2)}, u32[]{:S(2)}) %collective-permute-start.2) | collective-permute-done | bytes 1048608 | tf_op jit(solution)/shard_map/ppermute | solution.py:17
  137.0 2.6 collective-permute-done.3
  139.9 1.3 collective-permute-start.4
  141.2 23.9 %collective-permute-done.4 = f32[512,512]{1,0:T(8,128)S(1)} collective-permute-done((f32[512,512]{1,0:T(8,128)S(1)}, f32[512,512]{1,0:T(8,128)S(1)}, u32[]{:S(2)}, u32[]{:S(2)}) %collective-permute-start.4) | collective-permute-done | bytes 1048608 | tf_op jit(solution)/shard_map/ppermute | solution.py:17
  165.4 1.8 collective-permute-start.5
  167.2 22.6 %collective-permute-done.5 = f32[512,512]{1,0:T(8,128)S(1)} collective-permute-done((f32[512,512]{1,0:T(8,128)S(1)}, f32[512,512]{1,0:T(8,128)S(1)}, u32[]{:S(2)}, u32[]{:S(2)}) %collective-permute-start.5) | collective-permute-done | bytes 1048608 | tf_op jit(solution)/shard_map/ppermute | solution.py:17
  191.4 2.6 collective-permute-done.6
  194.2 1.3 collective-permute-start.7
  195.6 23.9 %collective-permute-done.7 = f32[512,512]{1,0:T(8,128)S(1)} collective-permute-done((f32[512,512]{1,0:T(8,128)S(1)}, f32[512,512]{1,0:T(8,128)S(1)}, u32[]{:S(2)}, u32[]{:S(2)}) %collective-permute-start.7) | collective-permute-done | bytes 1048608 | tf_op jit(solution)/shard_map/ppermute | solution.py:17
  219.7 1.8 collective-permute-start.8
  221.5 22.6 %collective-permute-done.8 = f32[512,512]{1,0:T(8,128)S(1)} collective-permute-done((f32[512,512]{1,0:T(8,128)S(1)}, f32[512,512]{1,0:T(8,128)S(1)}, u32[]{:S(2)}, u32[]{:S(2)}) %collective-permute-start.8) | collective-permute-done | bytes 1048608 | tf_op jit(solution)/shard_map/ppermute | solution.py:17
  244.4 1.6 fusion.8
  245.9 4.4 %all-to-all-start.2 = ((bf16[1,16,32,512]{3,2,0,1:T(8,128)(2,1)}), bf16[1,16,32,512]{3,2,0,1:T(8,128)(2,1)S(1)}, u32[]{:S(2)}, u32[]{:S(2)}) async-start(bf16[1,16,32,512]{3,2,0,1:T(8,128)(2,1)} %bitcast.5), calls=%async_computation.2 | async-start | bytes 1048576 | tf_op jit(solution)/shard_map/all_to_all | solution.py:102
  250.4 1.3 fusion.21
  251.8 1.2 broadcast_divide_fusion
  253.0 11.6 %all-to-all-done.2 = bf16[1,16,32,512]{3,2,0,1:T(8,128)(2,1)S(1)} async-done(((bf16[1,16,32,512]{3,2,0,1:T(8,128)(2,1)}), bf16[1,16,32,512]{3,2,0,1:T(8,128)(2,1)S(1)}, u32[]{:S(2)}, u32[]{:S(2)}) %all-to-all-start.2) | async-done | bytes 524320 | tf_op jit(solution)/shard_map/all_to_all | solution.py:102
  264.6 1.1 convert_multiply_fusion
  (42 shorter events, 10.6 us)
Async XLA Ops:
  0.6 4.4 %copy-start.2 = (s32[2]{0:T(128)S(1)}, s32[2]{0:T(128)}, u32[]{:S(2)}) copy-start(s32[2]{0:T(128)} %param.6) | copy-start | bytes 28
  0.6 4.5 %copy-start = (f32[8]{0:T(128)S(1)}, f32[8]{0:T(128)}, u32[]{:S(2)}) copy-start(f32[8]{0:T(128)} %param.7) | copy-start | bytes 100
  0.7 5.1 %copy-start.1 = (s32[4]{0:T(128)S(1)}, s32[4]{0:T(128)}, u32[]{:S(2)}) copy-start(s32[4]{0:T(128)} %param.5) | copy-start | bytes 52
  0.7 18.8 %all-to-all-start = ((bf16[1,2,2,256,512]{4,3,2,0,1:T(8,128)(2,1)}), bf16[1,2,2,256,512]{4,3,2,0,1:T(8,128)(2,1)S(1)}, u32[]{:S(2)}, u32[]{:S(2)}) async-start(bf16[1,2,2,256,512]{4,3,2,0,1:T(8,128)(2,1)} %bitcast.31), calls=%async_computation | async-start | bytes 2097152 | tf_op jit(solution)/shard_map/all_to_all | solution.py:73
  82.4 2.7 %collective-permute-start = (f32[512,512]{1,0:T(8,128)S(1)}, f32[512,512]{1,0:T(8,128)S(1)}, u32[]{:S(2)}, u32[]{:S(2)}) collective-permute-start(f32[512,512]{1,0:T(8,128)S(1)} %fusion.22), channel_id=1, source_target_pairs={{0,1},{1,0},{2,3},{3,2},{4,5},{5,4},{6,7},{7,6},{8,9},{9,8},{10,11... | collective-permute-start | bytes 3145736 | tf_op jit(solution)/shard_map/ppermute | solution.py:17
  85.3 25.3 %collective-permute-start.1 = (f32[512,512]{1,0:T(8,128)S(1)}, f32[512,512]{1,0:T(8,128)S(1)}, u32[]{:S(2)}, u32[]{:S(2)}) collective-permute-start(f32[512,512]{1,0:T(8,128)S(1)} %add.76), channel_id=1, source_target_pairs={{0,2},{1,3},{2,0},{3,1},{4,6},{5,7},{6,4},{7,5},{8,10},{9,11},{10,... | collective-permute-start | bytes 3145736 | tf_op jit(solution)/shard_map/ppermute | solution.py:17
  110.8 24.7 %collective-permute-start.2 = (f32[512,512]{1,0:T(8,128)S(1)}, f32[512,512]{1,0:T(8,128)S(1)}, u32[]{:S(2)}, u32[]{:S(2)}) collective-permute-start(f32[512,512]{1,0:T(8,128)S(1)} %add.77), channel_id=1, source_target_pairs={{0,4},{1,5},{2,6},{3,7},{4,0},{5,1},{6,2},{7,3},{8,12},{9,13},{10,... | collective-permute-start | bytes 3145736 | tf_op jit(solution)/shard_map/ppermute | solution.py:17
  137.0 2.7 %collective-permute-start.3 = (f32[512,512]{1,0:T(8,128)S(1)}, f32[512,512]{1,0:T(8,128)S(1)}, u32[]{:S(2)}, u32[]{:S(2)}) collective-permute-start(f32[512,512]{1,0:T(8,128)S(1)} %fusion.23), channel_id=1, source_target_pairs={{0,1},{1,0},{2,3},{3,2},{4,5},{5,4},{6,7},{7,6},{8,9},{9,8},{10,11... | collective-permute-start | bytes 3145736 | tf_op jit(solution)/shard_map/ppermute | solution.py:17
  139.9 25.3 %collective-permute-start.4 = (f32[512,512]{1,0:T(8,128)S(1)}, f32[512,512]{1,0:T(8,128)S(1)}, u32[]{:S(2)}, u32[]{:S(2)}) collective-permute-start(f32[512,512]{1,0:T(8,128)S(1)} %add.81), channel_id=1, source_target_pairs={{0,2},{1,3},{2,0},{3,1},{4,6},{5,7},{6,4},{7,5},{8,10},{9,11},{10,... | collective-permute-start | bytes 3145736 | tf_op jit(solution)/shard_map/ppermute | solution.py:17
  165.4 24.4 %collective-permute-start.5 = (f32[512,512]{1,0:T(8,128)S(1)}, f32[512,512]{1,0:T(8,128)S(1)}, u32[]{:S(2)}, u32[]{:S(2)}) collective-permute-start(f32[512,512]{1,0:T(8,128)S(1)} %add.82), channel_id=1, source_target_pairs={{0,4},{1,5},{2,6},{3,7},{4,0},{5,1},{6,2},{7,3},{8,12},{9,13},{10,... | collective-permute-start | bytes 3145736 | tf_op jit(solution)/shard_map/ppermute | solution.py:17
  191.3 2.7 %collective-permute-start.6 = (f32[512,512]{1,0:T(8,128)S(1)}, f32[512,512]{1,0:T(8,128)S(1)}, u32[]{:S(2)}, u32[]{:S(2)}) collective-permute-start(f32[512,512]{1,0:T(8,128)S(1)} %fusion.24), channel_id=1, source_target_pairs={{0,1},{1,0},{2,3},{3,2},{4,5},{5,4},{6,7},{7,6},{8,9},{9,8},{10,11... | collective-permute-start | bytes 3145736 | tf_op jit(solution)/shard_map/ppermute | solution.py:17
  194.2 25.3 %collective-permute-start.7 = (f32[512,512]{1,0:T(8,128)S(1)}, f32[512,512]{1,0:T(8,128)S(1)}, u32[]{:S(2)}, u32[]{:S(2)}) collective-permute-start(f32[512,512]{1,0:T(8,128)S(1)} %add.86), channel_id=1, source_target_pairs={{0,2},{1,3},{2,0},{3,1},{4,6},{5,7},{6,4},{7,5},{8,10},{9,11},{10,... | collective-permute-start | bytes 3145736 | tf_op jit(solution)/shard_map/ppermute | solution.py:17
  219.7 24.4 %collective-permute-start.8 = (f32[512,512]{1,0:T(8,128)S(1)}, f32[512,512]{1,0:T(8,128)S(1)}, u32[]{:S(2)}, u32[]{:S(2)}) collective-permute-start(f32[512,512]{1,0:T(8,128)S(1)} %add.87), channel_id=1, source_target_pairs={{0,4},{1,5},{2,6},{3,7},{4,0},{5,1},{6,2},{7,3},{8,12},{9,13},{10,... | collective-permute-start | bytes 3145736 | tf_op jit(solution)/shard_map/ppermute | solution.py:17
  245.9 18.7 %all-to-all-start.2 = ((bf16[1,16,32,512]{3,2,0,1:T(8,128)(2,1)}), bf16[1,16,32,512]{3,2,0,1:T(8,128)(2,1)S(1)}, u32[]{:S(2)}, u32[]{:S(2)}) async-start(bf16[1,16,32,512]{3,2,0,1:T(8,128)(2,1)} %bitcast.5), calls=%async_computation.2 | async-start | bytes 1048576 | tf_op jit(solution)/shard_map/all_to_all | solution.py:102
where the time goes:
time: 266 us
  waiting for transfers between devices  172 us (65%)
  blocking collectives  59.3 us (22%)
  starting transfers between devices  18.3 us (7%)
  other arithmetic  9.43 us (4%)
  matrix products  4.55 us (2%)
    ppermute x9, waiting for transfers between devices, partner(): lax.ppermute(shard, axis, [(i, i ^ 1 << stride) for i in range(lax.axis_s...  148 us
    psum x1, blocking collectives, share_scores(): return lax.psum((aligned, squares, norm_slots), ('domain', 'fsdp'))  39.8 us
    all_to_all x1, blocking collectives, body(): lax.all_to_all(scaled, 'fsdp', split_axis=0, concat_axis=1, tiled=True)  19.5 us
    all_to_all x1, waiting for transfers between devices, body(): lax.all_to_all(gradients.reshape(1, groups, per_domain, rows_src, columns...  12.7 us
    all_to_all x1, waiting for transfers between devices, body(): lax.all_to_all(finished.reshape(1, shards, sub_rows, columns), 'fsdp', sp...  11.6 us
    ppermute x9, starting transfers between devices, partner(): lax.ppermute(shard, axis, [(i, i ^ 1 << stride) for i in range(lax.axis_s...  9.5 us
  transfers between devices with their start and end apart: 11, of which 11 were waited for; matrix products, arithmetic and copies ran while one was open for 2% of the time, Pallas kernels for 0%

commit v1 on v0

--- a/solution.py
+++ b/solution.py
@@ -99,12 +99,18 @@
     start_rows = lax.all_to_all(scaled, "fsdp", split_axis=0, concat_axis=1, tiled=True)
     start_rows = lax.optimization_barrier(start_rows.reshape(own_rows, columns))
     finished = newton_steps(start_rows)
-    returned = lax.all_to_all(
-        finished.reshape(1, shards, sub_rows, columns),
-        "fsdp",
-        split_axis=1,
-        concat_axis=0,
-        tiled=True,
+    returned = jnp.concatenate(
+        lax.all_to_all(
+            jnp.stack(
+                jnp.split(
+                    finished.reshape(1, shards, sub_rows, columns), lax.axis_size("fsdp"), axis=1
+                )
+            ),
+            "fsdp",
+            0,
+            0,
+        ),
+        axis=0,
     )
     returned = returned.reshape(per_domain, rows_src, columns)
     updates = returned.astype(jnp.float32) * (MUON_SCALE * math.sqrt(full_rows))

time: 266 us -> 275 us (1.034)
  local copies, waits for them, and re-layouts: 0.45 us -> 10.3 us
    unnamed x6 -> x21, local copies, waits for them, and re-layouts: 0.01 us -> 9.27 us
where the time goes in v1:
time: 275 us
  waiting for transfers between devices  172 us (63%)
  blocking collectives  59.3 us (22%)
  starting transfers between devices  18.3 us (7%)
  local copies, waits for them, and re-layouts  10.3 us (4%)
  other arithmetic  9.43 us (3%)
  matrix products  3.76 us (1%)
    ppermute x9, waiting for transfers between devices, partner(): lax.ppermute(shard, axis, [(i, i ^ 1 << stride) for i in range(lax.axis_s...  148 us
    psum x1, blocking collectives, share_scores(): return lax.psum((aligned, squares, norm_slots), ('domain', 'fsdp'))  39.8 us
    all_to_all x1, blocking collectives, body(): lax.all_to_all(scaled, 'fsdp', split_axis=0, concat_axis=1, tiled=True)  19.5 us
    all_to_all x1, waiting for transfers between devices, body(): lax.all_to_all(gradients.reshape(1, groups, per_domain, rows_src, columns...  12.7 us
    all_to_all x1, waiting for transfers between devices, body(): lax.all_to_all(jnp.stack(jnp.split(finished.reshape(1, shards, sub_rows,...  11.6 us
    ppermute x9, starting transfers between devices, partner(): lax.ppermute(shard, axis, [(i, i ^ 1 << stride) for i in range(lax.axis_s...  9.5 us
    unnamed x21, local copies, waits for them, and re-layouts  9.27 us
  transfers between devices with their start and end apart: 11, of which 11 were waited for; matrix products, arithmetic and copies ran while one was open for 2% of the time, Pallas kernels for 0%

profile of v1, /device:TPU:0, one launch (start us, length us, event | category | flops | bytes accessed | tf_op | source)
XLA Modules:
  0.0 274.8 jit_solution(17265807208124331219)
XLA Ops:
  0.7 4.4 %all-to-all-start = ((bf16[1,2,2,256,512]{4,3,2,0,1:T(8,128)(2,1)}), bf16[1,2,2,256,512]{4,3,2,0,1:T(8,128)(2,1)S(1)}, u32[]{:S(2)}, u32[]{:S(2)}) async-start(bf16[1,2,2,256,512]{4,3,2,0,1:T(8,128)(2,1)} %bitcast.93), calls=%async_computation | async-start | bytes 2097152 | tf_op jit(solution)/shard_map/all_to_all | solution.py:73
  6.7 12.7 %all-to-all-done = bf16[1,2,2,256,512]{4,3,2,0,1:T(8,128)(2,1)S(1)} async-done(((bf16[1,2,2,256,512]{4,3,2,0,1:T(8,128)(2,1)}), bf16[1,2,2,256,512]{4,3,2,0,1:T(8,128)(2,1)S(1)}, u32[]{:S(2)}, u32[]{:S(2)}) %all-to-all-start) | async-done | bytes 1048608 | tf_op jit(solution)/shard_map/all_to_all | solution.py:73
  20.9 39.8 %all-reduce = (f32[4]{0:T(128)S(1)}, f32[2]{0:T(128)S(1)}, f32[2]{0:T(128)S(1)}) all-reduce(f32[4]{0:T(128)S(1)} %dynamic_update_slice.3, f32[2]{0:T(128)S(1)} %get-tuple-element.3, f32[2]{0:T(128)S(1)} %get-tuple-element.2), channel_id=1, replica_groups=mesh['domain'=2,'fsdp'=16] {'domain','fsdp'}, use_global_device_ids=true, to_apply=%region_5.6 | all-reduce | flops 8 | bytes 64 | tf_op jit(solution)/shard_map/psum | solution.py:55
  62.4 19.5 %all_to_all.23 = bf16[16,1,32,512]{3,2,1,0:T(8,128)(2,1)S(1)} all-to-all(bf16[16,1,32,512]{3,2,1,0:T(8,128)(2,1)S(1)} %divide_convert_fusion), channel_id=1, replica_groups=mesh['domain'=2,'fsdp'=16] {'fsdp'}, dimensions={0} | all-to-all | bytes 1048576 | tf_op jit(solution)/shard_map/all_to_all | solution.py:99
  82.6 2.5 collective-permute-done
  85.3 1.1 collective-permute-start.1
  86.4 24.2 %collective-permute-done.1 = f32[512,512]{1,0:T(8,128)S(1)} collective-permute-done((f32[512,512]{1,0:T(8,128)S(1)}, f32[512,512]{1,0:T(8,128)S(1)}, u32[]{:S(2)}, u32[]{:S(2)}) %collective-permute-start.1) | collective-permute-done | bytes 1048608 | tf_op jit(solution)/shard_map/ppermute | solution.py:17
  110.8 1.8 collective-permute-start.2
  112.6 22.8 %collective-permute-done.2 = f32[512,512]{1,0:T(8,128)S(1)} collective-permute-done((f32[512,512]{1,0:T(8,128)S(1)}, f32[512,512]{1,0:T(8,128)S(1)}, u32[]{:S(2)}, u32[]{:S(2)}) %collective-permute-start.2) | collective-permute-done | bytes 1048608 | tf_op jit(solution)/shard_map/ppermute | solution.py:17
  137.0 2.6 collective-permute-done.3
  139.9 1.3 collective-permute-start.4
  141.2 23.9 %collective-permute-done.4 = f32[512,512]{1,0:T(8,128)S(1)} collective-permute-done((f32[512,512]{1,0:T(8,128)S(1)}, f32[512,512]{1,0:T(8,128)S(1)}, u32[]{:S(2)}, u32[]{:S(2)}) %collective-permute-start.4) | collective-permute-done | bytes 1048608 | tf_op jit(solution)/shard_map/ppermute | solution.py:17
  165.4 1.8 collective-permute-start.5
  167.2 22.6 %collective-permute-done.5 = f32[512,512]{1,0:T(8,128)S(1)} collective-permute-done((f32[512,512]{1,0:T(8,128)S(1)}, f32[512,512]{1,0:T(8,128)S(1)}, u32[]{:S(2)}, u32[]{:S(2)}) %collective-permute-start.5) | collective-permute-done | bytes 1048608 | tf_op jit(solution)/shard_map/ppermute | solution.py:17
  191.4 2.6 collective-permute-done.6
  194.2 1.3 collective-permute-start.7
  195.6 23.9 %collective-permute-done.7 = f32[512,512]{1,0:T(8,128)S(1)} collective-permute-done((f32[512,512]{1,0:T(8,128)S(1)}, f32[512,512]{1,0:T(8,128)S(1)}, u32[]{:S(2)}, u32[]{:S(2)}) %collective-permute-start.7) | collective-permute-done | bytes 1048608 | tf_op jit(solution)/shard_map/ppermute | solution.py:17
  219.7 1.8 collective-permute-start.8
  221.5 22.6 %collective-permute-done.8 = f32[512,512]{1,0:T(8,128)S(1)} collective-permute-done((f32[512,512]{1,0:T(8,128)S(1)}, f32[512,512]{1,0:T(8,128)S(1)}, u32[]{:S(2)}, u32[]{:S(2)}) %collective-permute-start.8) | collective-permute-done | bytes 1048608 | tf_op jit(solution)/shard_map/ppermute | solution.py:17
  255.0 4.4 %all-to-all-start.2 = ((bf16[16,1,1,32,512]{4,3,2,1,0:T(8,128)(2,1)}), bf16[16,1,1,32,512]{4,3,2,1,0:T(8,128)(2,1)S(1)}, u32[]{:S(2)}, u32[]{:S(2)}) async-start(bf16[16,1,1,32,512]{4,3,2,1,0:T(8,128)(2,1)} %constant_dynamic-update-slice_fusion), calls=%async_computation.2 | async-start | bytes 1048576 | tf_op jit(solution)/shard_map/all_to_all | solution.py:103
  259.5 1.3 fusion.21
  260.9 1.2 broadcast_divide_fusion
  262.1 11.6 %all-to-all-done.2 = bf16[16,1,1,32,512]{4,3,2,1,0:T(8,128)(2,1)S(1)} async-done(((bf16[16,1,1,32,512]{4,3,2,1,0:T(8,128)(2,1)}), bf16[16,1,1,32,512]{4,3,2,1,0:T(8,128)(2,1)S(1)}, u32[]{:S(2)}, u32[]{:S(2)}) %all-to-all-start.2) | async-done | bytes 524320 | tf_op jit(solution)/shard_map/all_to_all | solution.py:103
  273.7 1.1 convert_multiply_fusion
  (58 shorter events, 20.2 us)
Async XLA Ops:
  0.6 4.4 %copy-start.2 = (s32[2]{0:T(128)S(1)}, s32[2]{0:T(128)}, u32[]{:S(2)}) copy-start(s32[2]{0:T(128)} %param.6) | copy-start | bytes 28
  0.6 4.5 %copy-start = (f32[8]{0:T(128)S(1)}, f32[8]{0:T(128)}, u32[]{:S(2)}) copy-start(f32[8]{0:T(128)} %param.7) | copy-start | bytes 100
  0.7 5.1 %copy-start.1 = (s32[4]{0:T(128)S(1)}, s32[4]{0:T(128)}, u32[]{:S(2)}) copy-start(s32[4]{0:T(128)} %param.5) | copy-start | bytes 52
  0.7 18.8 %all-to-all-start = ((bf16[1,2,2,256,512]{4,3,2,0,1:T(8,128)(2,1)}), bf16[1,2,2,256,512]{4,3,2,0,1:T(8,128)(2,1)S(1)}, u32[]{:S(2)}, u32[]{:S(2)}) async-start(bf16[1,2,2,256,512]{4,3,2,0,1:T(8,128)(2,1)} %bitcast.93), calls=%async_computation | async-start | bytes 2097152 | tf_op jit(solution)/shard_map/all_to_all | solution.py:73
  82.4 2.7 collective-permute-start
  85.3 25.3 %collective-permute-start.1 = (f32[512,512]{1,0:T(8,128)S(1)}, f32[512,512]{1,0:T(8,128)S(1)}, u32[]{:S(2)}, u32[]{:S(2)}) collective-permute-start(f32[512,512]{1,0:T(8,128)S(1)} %add.76), channel_id=1, source_target_pairs={{0,2},{1,3},{2,0},{3,1},{4,6},{5,7},{6,4},{7,5},{8,10},{9,11},{10,... | collective-permute-start | bytes 3145736 | tf_op jit(solution)/shard_map/ppermute | solution.py:17
  110.8 24.7 %collective-permute-start.2 = (f32[512,512]{1,0:T(8,128)S(1)}, f32[512,512]{1,0:T(8,128)S(1)}, u32[]{:S(2)}, u32[]{:S(2)}) collective-permute-start(f32[512,512]{1,0:T(8,128)S(1)} %add.77), channel_id=1, source_target_pairs={{0,4},{1,5},{2,6},{3,7},{4,0},{5,1},{6,2},{7,3},{8,12},{9,13},{10,... | collective-permute-start | bytes 3145736 | tf_op jit(solution)/shard_map/ppermute | solution.py:17
  137.0 2.7 collective-permute-start.3
  139.9 25.3 %collective-permute-start.4 = (f32[512,512]{1,0:T(8,128)S(1)}, f32[512,512]{1,0:T(8,128)S(1)}, u32[]{:S(2)}, u32[]{:S(2)}) collective-permute-start(f32[512,512]{1,0:T(8,128)S(1)} %add.81), channel_id=1, source_target_pairs={{0,2},{1,3},{2,0},{3,1},{4,6},{5,7},{6,4},{7,5},{8,10},{9,11},{10,... | collective-permute-start | bytes 3145736 | tf_op jit(solution)/shard_map/ppermute | solution.py:17
  165.4 24.4 %collective-permute-start.5 = (f32[512,512]{1,0:T(8,128)S(1)}, f32[512,512]{1,0:T(8,128)S(1)}, u32[]{:S(2)}, u32[]{:S(2)}) collective-permute-start(f32[512,512]{1,0:T(8,128)S(1)} %add.82), channel_id=1, source_target_pairs={{0,4},{1,5},{2,6},{3,7},{4,0},{5,1},{6,2},{7,3},{8,12},{9,13},{10,... | collective-permute-start | bytes 3145736 | tf_op jit(solution)/shard_map/ppermute | solution.py:17
  191.3 2.7 collective-permute-start.6
  194.2 25.3 %collective-permute-start.7 = (f32[512,512]{1,0:T(8,128)S(1)}, f32[512,512]{1,0:T(8,128)S(1)}, u32[]{:S(2)}, u32[]{:S(2)}) collective-permute-start(f32[512,512]{1,0:T(8,128)S(1)} %add.86), channel_id=1, source_target_pairs={{0,2},{1,3},{2,0},{3,1},{4,6},{5,7},{6,4},{7,5},{8,10},{9,11},{10,... | collective-permute-start | bytes 3145736 | tf_op jit(solution)/shard_map/ppermute | solution.py:17
  219.7 24.4 %collective-permute-start.8 = (f32[512,512]{1,0:T(8,128)S(1)}, f32[512,512]{1,0:T(8,128)S(1)}, u32[]{:S(2)}, u32[]{:S(2)}) collective-permute-start(f32[512,512]{1,0:T(8,128)S(1)} %add.87), channel_id=1, source_target_pairs={{0,4},{1,5},{2,6},{3,7},{4,0},{5,1},{6,2},{7,3},{8,12},{9,13},{10,... | collective-permute-start | bytes 3145736 | tf_op jit(solution)/shard_map/ppermute | solution.py:17
  255.0 18.7 %all-to-all-start.2 = ((bf16[16,1,1,32,512]{4,3,2,1,0:T(8,128)(2,1)}), bf16[16,1,1,32,512]{4,3,2,1,0:T(8,128)(2,1)S(1)}, u32[]{:S(2)}, u32[]{:S(2)}) async-start(bf16[16,1,1,32,512]{4,3,2,1,0:T(8,128)(2,1)} %constant_dynamic-update-slice_fusion), calls=%async_computation.2 | async-start | bytes 1048576 | tf_op jit(solution)/shard_map/all_to_all | solution.py:103
